TPU v7x, 32 devices: a whole 2x2x4 slice. The times are simulated.
32 devices in a mesh: sph: 8 (over z, core), fit: 4 (over y, x).
Axes of the slice: x: 2, y: 2, z: 4, core: 2. Of those that a mesh axis runs over, the one named last changes fastest.
Arguments:
- tiles: bfloat16 [1024, 163840], P('fit', 'sph'), may hold values from -0.1875 to 0.1875
- coefs: bfloat16 [16, 1024], P(None, 'fit'), may hold values from -6 to 6
- centres: float32 [3, 512], P(None, ('sph', 'fit'))
- radii: float32 [512], P(('sph', 'fit')), may hold values from 1 to 1.6
- neighbours: int32 [512, 16], P(('sph', 'fit')), may hold values from 0 to 511, as said below
- counts: int32 [512], P(('sph', 'fit')), may hold values from 1 to 16
Outputs:
- moments: float32 [512, 16, 49], P(('sph', 'fit'))
- fock: float32 [16, 1024], P(None, 'fit')
Inputs may be any that keep to these rules, and one draw needn't show every extreme that they name: `neighbours`: every entry j of row i satisfies |j - i| <= 8; the first counts[i] entries of a row are distinct and differ from i, the rest equal i.
All inputs are finite; a program needn't handle non-finite values.
Results may differ from a plain program's by a relative error of at most 0.00086.
Values may be sent and summed in bfloat16 or wider, within the bound.
No kernel may reach another device: no remote copies, remote signals or barrier semaphores. Data moves between devices by JAX's collectives and lax.ppermute only.
A program may use at most 192 MiB of HBM per device.

v0:
```python
import math
import jax
import jax.numpy as jnp
from jax import lax
from jax.sharding import PartitionSpec as P

DEGREE = 6
NTH = 16
NPHI = 20
NG = 320
NDENS = 16
band = 0.1


def with_halo(array, sides, width):
    for axis, dim in sides:
        count, length = (lax.axis_size(axis), array.shape[dim])
        up = [(i, (i + 1) % count) for i in range(count - 1)]
        down = [(j, i) for i, j in up]
        last = lax.slice_in_dim(array, length - width, length, axis=dim)
        initial = lax.slice_in_dim(array, 0, width, axis=dim)
        before = lax.ppermute(last, axis, up)
        after = lax.ppermute(initial, axis, down)
        array = jnp.concatenate([before, array, after], axis=dim)
    return array


def solid(coord_x, coord_y, coord_z):
    radius_squared = coord_x * coord_x + coord_y * coord_y + coord_z * coord_z
    cos_part = [jnp.ones_like(coord_x)]
    sin_part = [jnp.zeros_like(coord_x)]
    for harmonic_order in range(1, DEGREE + 1):
        cprev = cos_part[-1]
        sprev = sin_part[-1]
        cos_part.append(cprev * coord_x - sprev * coord_y)
        sin_part.append(cprev * coord_y + sprev * coord_x)
    result = [None] * (DEGREE + 1) ** 2
    for harmonic_order in range(DEGREE + 1):
        dfact = 1.0
        for odd in range(1, 2 * harmonic_order, 2):
            dfact = dfact * odd
        lower_term = None
        current = dfact * jnp.ones_like(coord_x)
        for harmonic_degree in range(harmonic_order, DEGREE + 1):
            if harmonic_degree > harmonic_order:
                next_term = (2 * harmonic_degree - 1) * coord_z * current
                if lower_term is not None:
                    next_term = (
                        next_term
                        - (harmonic_degree + harmonic_order - 1) * radius_squared * lower_term
                    )
                lower_term = current
                current = next_term / (harmonic_degree - harmonic_order)
            scale = math.sqrt(
                (2 * harmonic_degree + 1)
                / (4 * math.pi)
                * math.factorial(harmonic_degree - harmonic_order)
                / math.factorial(harmonic_degree + harmonic_order)
            )
            if harmonic_order == 0:
                result[harmonic_degree * harmonic_degree + harmonic_degree] = scale * current
            else:
                result[harmonic_degree * harmonic_degree + harmonic_degree + harmonic_order] = (
                    math.sqrt(2.0) * scale * current * cos_part[harmonic_order]
                )
                result[harmonic_degree * harmonic_degree + harmonic_degree - harmonic_order] = (
                    math.sqrt(2.0) * scale * current * sin_part[harmonic_order]
                )
    return result


def grid_tables():
    polar_index = jnp.arange(NTH, dtype=jnp.float32)
    polar_nodes = -1.0 + (2.0 * polar_index + 1.0) / NTH
    angles = (jnp.arange(NPHI, dtype=jnp.float32) + 0.5) * (2.0 * math.pi / NPHI)
    cosines = jnp.repeat(polar_nodes, NPHI)
    sines = jnp.sqrt(1.0 - cosines * cosines)
    azimuth = jnp.tile(angles, NTH)
    dirs = jnp.stack([sines * jnp.cos(azimuth), sines * jnp.sin(azimuth), cosines])
    weights = jnp.full((NTH * NPHI,), 4.0 * math.pi / (NTH * NPHI), dtype=jnp.float32)
    ysurf = jnp.stack(solid(dirs[0], dirs[1], dirs[2]))
    levels = jnp.asarray(
        [
            float(harmonic_degree)
            for harmonic_degree in range(DEGREE + 1)
            for harmonic_order in range(2 * harmonic_degree + 1)
        ],
        dtype=jnp.float32,
    )
    couple = 4.0 * math.pi / (2.0 * levels + 1.0)
    invert = (2.0 * levels + 1.0) / (4.0 * math.pi)
    return (dirs, weights, ysurf, couple, invert)


def block_basis(own, near, valid, dirs, couple):
    centre = own[:3]
    radius = own[3]
    offset = centre[:, :, None] - near[:3]
    near_rad = jnp.where(valid > 0, near[3], 1.0)
    vec = (offset[:, :, :, None] + radius[None, :, None, None] * dirs[:, None, None, :]) / near_rad[
        None, :, :, None
    ]
    dist = jnp.sqrt(jnp.sum(vec * vec, axis=0))
    ramp = jnp.clip((1.0 - dist) / band, 0.0, 1.0)
    switch = ramp * ramp * (3.0 - 2.0 * ramp) * valid[:, :, None]
    harm = jnp.stack(solid(vec[0], vec[1], vec[2]), axis=2)
    basis = harm * couple[None, None, :, None] * switch[:, :, None, :]
    uncovered = jnp.maximum(0.0, 1.0 - jnp.sum(switch, axis=1))
    return (basis, uncovered)


def block_rhs(weighted, uncovered, potential):
    return -jnp.einsum(
        "lp,sdp->sdl", weighted, uncovered[:, None, :] * potential, precision=lax.Precision.HIGHEST
    )


def block_sweep(basis, weighted, invert, rhs, near_moments):
    field = jnp.einsum("sklp,skdl->sdp", basis, near_moments, precision=lax.Precision.HIGHEST)
    proj = jnp.einsum("lp,sdp->sdl", weighted, field, precision=lax.Precision.HIGHEST)
    return invert[None, None, :] * (rhs + proj)


def block_charges(ysurf, weights, uncovered, moments):
    surface = jnp.einsum("lp,sdl->sdp", ysurf, moments, precision=lax.Precision.HIGHEST)
    return (surface * (weights[None, None, :] * uncovered[:, None, :])).astype(jnp.bfloat16)


def body(tiles, coefs, centres, radii, neighbours, counts):
    spheres = neighbours.shape[0]
    slots = neighbours.shape[1]
    reach = slots // 2
    aux_local = tiles.shape[0]
    block = tiles.shape[1] // NG
    dirs, weights, ysurf, couple, invert = grid_tables()
    weighted = ysurf * weights[None, :]
    tile_three = tiles.reshape(aux_local, block, NG)
    fit_index = lax.axis_index("fit")
    first_sphere = (lax.axis_index("sph") * lax.axis_size("fit") + fit_index) * spheres
    whole = jnp.einsum("da,acn->cdn", coefs, tile_three, preferred_element_type=jnp.float32)
    whole = lax.psum(whole.reshape(block, NDENS * NG), "fit")
    potential = lax.dynamic_slice_in_dim(whole, fit_index * spheres, spheres, 0)
    potential = potential.reshape(spheres, NDENS, NG)
    geometry = jnp.concatenate([centres, radii[None, :]], axis=0)
    valid = (jnp.arange(slots)[None, :] < counts[:, None]).astype(jnp.float32)
    near_geo = with_halo(geometry, ((("sph", "fit"), 1),), reach)
    local = jnp.clip(neighbours - (first_sphere - reach), 0, spheres + 2 * reach - 1)
    basis, uncovered = block_basis(geometry, near_geo[:, local], valid, dirs, couple)
    rhs = block_rhs(weighted, uncovered, potential)
    moments = invert[None, None, :] * rhs
    for sweep in range(2):
        near_state = with_halo(moments, ((("sph", "fit"), 0),), reach)
        moments = block_sweep(basis, weighted, invert, rhs, near_state[local])
    charges = block_charges(ysurf, weights, uncovered, moments).reshape(spheres, NDENS * NG)
    piece = lax.all_gather(charges, "fit", axis=0, tiled=True)
    rows = piece.shape[0]
    shaped = piece.reshape(rows, NDENS, NG)
    partial_fock = lax.dot_general(
        shaped, tile_three, (((0, 2), (1, 2)), ((), ())), preferred_element_type=jnp.float32
    )
    fock = lax.psum(partial_fock, "sph")
    return (moments, fock)


def solution(mesh):
    placed = (
        P("fit", "sph"),
        P(None, "fit"),
        P(None, ("sph", "fit")),
        P(("sph", "fit")),
        P(("sph", "fit"), None),
        P(("sph", "fit")),
    )
    return jax.shard_map(
        body,
        mesh=mesh,
        in_specs=placed,
        out_specs=(P(("sph", "fit"), None, None), P(None, "fit")),
        check_vma=False,
    )
```

profile of v0, /device:TPU:0, one launch (start us, length us, event | category | flops | bytes accessed | tf_op | source)
XLA Modules:
  0.0 242.6 jit_solution(9293991548820046019)
XLA Ops:
  8.0 4.8 %collective-permute-start = (f32[4,8]{1,0:T(4,128)S(1)}, f32[4,8]{1,0:T(4,128)S(1)}, u32[]{:S(2)}, u32[]{:S(2)}) collective-permute-start(f32[4,8]{1,0:T(4,128)S(1)} %get-tuple-element.90), channel_id=1, source_target_pairs={{0,1},{1,2},{2,3},{3,4},{4,5},{5,6},{6,7},{7,8},{8,9},{9,10},{10,1... | collective-permute-start | bytes 392 | tf_op jit(solution)/shard_map/ppermute | solution.py:22
  12.9 1.4 collective-permute-start.1
  14.3 13.7 %copy.25 = bf16[256,20480]{0,1:T(8,128)(2,1)} copy(bf16[256,20480]{1,0:T(8,128)(2,1)} %param.7) | data formatting | bytes 20971520 | tf_op args[0]
  28.0 7.1 %convolution_bitcast_fusion = f32[64,16,320]{2,1,0:T(8,128)S(1)} fusion(bf16[256,64,320]{0,2,1:T(8,128)(2,1)} %bitcast.208, bf16[16,256]{1,0:T(8,128)(2,1)S(1)} %copy-done), kind=kOutput, calls=%fused_computation.8 | convolution fusion | flops 167772160 | bytes 11804672 | tf_op jit(solution)/shard_map/da,acn->cdn/dot_general | solution.py:140
  35.1 1.6 reshape.3985
  65.7 1.1 multiply_dynamic-update-slice_fusion.18
  66.7 1.1 multiply_dynamic-update-slice_fusion.17
  74.8 1.0 multiply_dynamic-update-slice_fusion.8
  75.8 1.1 multiply_dynamic-update-slice_fusion.7
  76.9 1.1 multiply_dynamic-update-slice_fusion.6
  78.0 1.1 multiply_dynamic-update-slice_fusion.5
  79.4 1.0 multiply_dynamic-update-slice_fusion.4
  83.9 11.8 %all-reduce.2.cloned.1.call-done = f32[64,5120]{1,0:T(8,128)} async-done(((f32[64,5120]{1,0:T(8,128)}), f32[64,5120]{1,0:T(8,128)}) %all-reduce.2.cloned.1.call-update) | async-done | bytes 1310736 | tf_op jit(solution)/shard_map/psum | solution.py:141
  97.4 3.4 %collective-permute-start.2 = (f32[8,16,49]{2,1,0:T(8,128)S(1)}, f32[8,16,49]{2,1,0:T(8,128)S(1)}, u32[]{:S(2)}, u32[]{:S(2)}) collective-permute-start(f32[8,16,49]{2,1,0:T(8,128)S(1)} %get-tuple-element.58), channel_id=1, source_target_pairs={{0,1},{1,2},{2,3},{3,4},{4,5},{5,6},{6,7},{7,8},{8,9},{9,10},{10,1... | collective-permute-start | bytes 75272 | tf_op jit(solution)/shard_map/ppermute | solution.py:22
  100.7 1.5 collective-permute-start.3
  102.2 15.1 %multiply_multiply_fusion = f32[16,16,49,320]{3,1,2,0:T(8,128)} fusion(f32[16,16,49,320]{3,1,2,0:T(8,128)} %multiply_dynamic-update-slice_fusion, f32[16,16,320]{2,1,0:T(8,128)S(1)} %get-tuple-element.55, f32[49]{0:T(128)S(1)} %copy-done.8), kind=kLoop, calls=%fused_computation.7 | loop fusion | flops 8028160 | bytes 32440516 | tf_op jit(solution)/shard_map/mul | solution.py:107
  118.4 28.6 %fusion.4 = f32[16,16,320]{2,1,0:T(8,128)S(1)} fusion(f32[16,16,16,49]{3,2,1,0:T(8,128)S(1)} %bitcast.211, f32[16,16,49,320]{3,1,2,0:T(8,128)} %multiply_multiply_fusion), kind=kOutput, calls=%fused_computation.10 | convolution fusion | flops 770703360 | bytes 17186816 | tf_op jit(solution)/shard_map/sklp,skdl->sdp/dot_general | solution.py:119
  147.5 4.5 %collective-permute-start.4 = (f32[8,16,49]{2,1,0:T(8,128)S(1)}, f32[8,16,49]{2,1,0:T(8,128)S(1)}, u32[]{:S(2)}, u32[]{:S(2)}) collective-permute-start(f32[8,16,49]{2,1,0:T(8,128)S(1)} %get-tuple-element.56), channel_id=1, source_target_pairs={{0,1},{1,2},{2,3},{3,4},{4,5},{5,6},{6,7},{7,8},{8,9},{9,10},{10,1... | collective-permute-start | bytes 75272 | tf_op jit(solution)/shard_map/ppermute | solution.py:22
  152.1 1.5 collective-permute-start.5
  153.9 4.6 %collective-permute-done.5 = f32[8,16,49]{2,1,0:T(8,128)S(1)} collective-permute-done((f32[8,16,49]{2,1,0:T(8,128)S(1)}, f32[8,16,49]{2,1,0:T(8,128)S(1)}, u32[]{:S(2)}, u32[]{:S(2)}) %collective-permute-start.5) | collective-permute-done | bytes 25120 | tf_op jit(solution)/shard_map/ppermute | solution.py:23
  159.6 28.6 %fusion.7 = f32[16,16,320]{2,1,0:T(8,128)S(1)} fusion(f32[16,16,16,49]{3,2,1,0:T(8,128)S(1)} %bitcast.210, f32[16,16,49,320]{3,1,2,0:T(8,128)} %multiply_multiply_fusion), kind=kOutput, calls=%fused_computation.11 | convolution fusion | flops 770703360 | bytes 17186816 | tf_op jit(solution)/shard_map/sklp,skdl->sdp/dot_general | solution.py:119
  189.3 13.8 %all_gather.3 = bf16[64,5120]{1,0:T(8,128)(2,1)S(1)} all-gather(bf16[16,5120]{1,0:T(8,128)(2,1)S(1)} %reshape.3987), channel_id=1, replica_groups=mesh['sph'=8,'fit'=4] {'fit'}, dimensions={0}, use_global_device_ids=true | all-gather | bytes 819200 | tf_op jit(solution)/shard_map/all_gather | solution.py:155
  203.7 5.5 %convolution_bitcast_fusion.1 = f32[16,256]{1,0:T(8,128)S(1)} fusion(bf16[64,16,320]{2,1,0:T(8,128)(2,1)S(1)} %reshape.3988, bf16[256,64,320]{0,2,1:T(8,128)(2,1)} %bitcast.209), kind=kOutput, calls=%fused_computation.20 | convolution fusion | flops 167772160 | bytes 11157504 | tf_op jit(solution)/shard_map/dot_general | solution.py:158
  209.2 26.5 %psum.15 = f32[16,256]{1,0:T(8,128)} all-reduce(f32[16,256]{1,0:T(8,128)S(1)} %convolution_bitcast_fusion.1), channel_id=1, replica_groups=mesh['sph'=8,'fit'=4] {'sph'}, use_global_device_ids=true, to_apply=%region_3.4 | all-reduce | flops 4096 | bytes 32768 | tf_op jit(solution)/shard_map/psum | solution.py:161
  (117 shorter events, 46.7 us)
Async XLA Ops:
  7.2 20.8 %copy-start = (bf16[16,256]{1,0:T(8,128)(2,1)S(1)}, bf16[16,256]{1,0:T(8,128)(2,1)}, u32[]{:S(2)}) copy-start(bf16[16,256]{1,0:T(8,128)(2,1)} %param.8) | copy-start | bytes 24580
  7.2 88.5 %all-reduce.2.cloned.1.call-start = ((), (), s32[]{:S(2)}) async-start(), calls=%async_computation | async-start | bytes 2621440 | tf_op jit(solution)/shard_map/psum | solution.py:141
  8.0 30.6 %collective-permute-start = (f32[4,8]{1,0:T(4,128)S(1)}, f32[4,8]{1,0:T(4,128)S(1)}, u32[]{:S(2)}, u32[]{:S(2)}) collective-permute-start(f32[4,8]{1,0:T(4,128)S(1)} %get-tuple-element.90), channel_id=1, source_target_pairs={{0,1},{1,2},{2,3},{3,4},{4,5},{5,6},{6,7},{7,8},{8,9},{9,10},{10,1... | collective-permute-start | bytes 392 | tf_op jit(solution)/shard_map/ppermute | solution.py:22
  12.8 25.1 %copy-start.5 = (f32[16]{0:T(128)S(1)}, f32[16]{0:T(128)}, u32[]{:S(2)}) copy-start(f32[16]{0:T(128)} %param.10) | copy-start | bytes 196
  12.9 25.2 %copy-start.4 = (s32[16,16]{1,0:T(8,128)S(1)}, s32[16,16]{1,0:T(8,128)}, u32[]{:S(2)}) copy-start(s32[16,16]{1,0:T(8,128)} %param.11) | copy-start | bytes 3076
  12.9 25.3 %copy-start.7 = (s32[16]{0:T(128)S(1)}, s32[16]{0:T(128)}, u32[]{:S(2)}) copy-start(s32[16]{0:T(128)} %param.12) | copy-start | bytes 196
  12.9 25.8 %copy-start.3 = (f32[3,16]{1,0:T(4,128)S(1)}, f32[3,16]{1,0:T(4,128)}, u32[]{:S(2)}) copy-start(f32[3,16]{1,0:T(4,128)} %param.9) | copy-start | bytes 580
  12.9 25.7 %collective-permute-start.1 = (f32[4,8]{1,0:T(4,128)S(1)}, f32[4,8]{1,0:T(4,128)S(1)}, u32[]{:S(2)}, u32[]{:S(2)}) collective-permute-start(f32[4,8]{1,0:T(4,128)S(1)} %get-tuple-element.91), channel_id=1, source_target_pairs={{1,0},{2,1},{3,2},{4,3},{5,4},{6,5},{7,6},{8,7},{9,8},{10,9},{11,1... | collective-permute-start | bytes 392 | tf_op jit(solution)/shard_map/ppermute | solution.py:23
  62.0 34.9 %copy-start.6 = (f32[49]{0:T(128)S(1)}, f32[49]{0:T(128)}, u32[]{:S(2)}) copy-start(f32[49]{0:T(128)} %constant.272) | copy-start | bytes 592
  62.0 40.3 %copy-start.8 = (f32[49]{0:T(128)S(1)}, f32[49]{0:T(128)}, u32[]{:S(2)}) copy-start(f32[49]{0:T(128)} %constant.273) | copy-start | bytes 592
  97.4 20.0 %collective-permute-start.2 = (f32[8,16,49]{2,1,0:T(8,128)S(1)}, f32[8,16,49]{2,1,0:T(8,128)S(1)}, u32[]{:S(2)}, u32[]{:S(2)}) collective-permute-start(f32[8,16,49]{2,1,0:T(8,128)S(1)} %get-tuple-element.58), channel_id=1, source_target_pairs={{0,1},{1,2},{2,3},{3,4},{4,5},{5,6},{6,7},{7,8},{8,9},{9,10},{10,1... | collective-permute-start | bytes 75272 | tf_op jit(solution)/shard_map/ppermute | solution.py:22
  100.7 16.6 %collective-permute-start.3 = (f32[8,16,49]{2,1,0:T(8,128)S(1)}, f32[8,16,49]{2,1,0:T(8,128)S(1)}, u32[]{:S(2)}, u32[]{:S(2)}) collective-permute-start(f32[8,16,49]{2,1,0:T(8,128)S(1)} %get-tuple-element.59), channel_id=1, source_target_pairs={{1,0},{2,1},{3,2},{4,3},{5,4},{6,5},{7,6},{8,7},{9,8},{10,9},{11,1... | collective-permute-start | bytes 75272 | tf_op jit(solution)/shard_map/ppermute | solution.py:23
  147.5 6.4 %collective-permute-start.4 = (f32[8,16,49]{2,1,0:T(8,128)S(1)}, f32[8,16,49]{2,1,0:T(8,128)S(1)}, u32[]{:S(2)}, u32[]{:S(2)}) collective-permute-start(f32[8,16,49]{2,1,0:T(8,128)S(1)} %get-tuple-element.56), channel_id=1, source_target_pairs={{0,1},{1,2},{2,3},{3,4},{4,5},{5,6},{6,7},{7,8},{8,9},{9,10},{10,1... | collective-permute-start | bytes 75272 | tf_op jit(solution)/shard_map/ppermute | solution.py:22
  152.1 6.4 %collective-permute-start.5 = (f32[8,16,49]{2,1,0:T(8,128)S(1)}, f32[8,16,49]{2,1,0:T(8,128)S(1)}, u32[]{:S(2)}, u32[]{:S(2)}) collective-permute-start(f32[8,16,49]{2,1,0:T(8,128)S(1)} %get-tuple-element.57), channel_id=1, source_target_pairs={{1,0},{2,1},{3,2},{4,3},{5,4},{6,5},{7,6},{8,7},{9,8},{10,9},{11,1... | collective-permute-start | bytes 75272 | tf_op jit(solution)/shard_map/ppermute | solution.py:23
  159.5 76.2 %copy-start.1 = (bf16[16,256]{1,0:T(8,128)(2,1)S(1)}, bf16[16,256]{1,0:T(8,128)(2,1)}, u32[]{:S(2)}) copy-start(bf16[16,256]{1,0:T(8,128)(2,1)} %param.8) | copy-start | bytes 24580
  188.6 47.1 %copy-start.2 = (f32[16,16,49]{2,1,0:T(8,128)}, f32[16,16,49]{2,1,0:T(8,128)S(1)}, u32[]{:S(2)}) copy-start(f32[16,16,49]{2,1,0:T(8,128)S(1)} %fusion.11) | copy-start | bytes 150532
Sparse Core Ops, SparseCore 0:
  36.8 58.9 all-reduce.1
where the time goes:
time: 243 us
  matrix products  71.6 us (29%)
  other arithmetic  60.6 us (25%)
  blocking collectives  40.3 us (17%)
  local copies, waits for them, and re-layouts  21.7 us (9%)
  starting transfers between devices  17.2 us (7%)
  waiting for transfers between devices  16.7 us (7%)
  between operations  14.4 us (6%)
    dot_general x2, matrix products, block_sweep(): jnp.einsum('sklp,skdl->sdp', basis, near_moments, precision=lax.Precision...  57.2 us
    unnamed x47, other arithmetic  42.6 us
    psum x1, blocking collectives, body(): fock = lax.psum(partial_fock, 'sph')  26.5 us
    mul x1, other arithmetic, block_basis(): basis = harm * couple[None, None, :, None] * switch[:, :, None, :]  15.1 us
    unnamed x20, local copies, waits for them, and re-layouts  14.5 us
    all_gather x1, blocking collectives, body(): piece = lax.all_gather(charges, 'fit', axis=0, tiled=True)  13.8 us
    ppermute x3, starting transfers between devices, with_halo(): before = lax.ppermute(last, axis, up)  12.8 us
    psum x1, waiting for transfers between devices, body(): whole = lax.psum(whole.reshape(block, NDENS * NG), 'fit')  11.8 us
  transfers between devices with their start and end apart: 7, of which 3 were waited for; matrix products, arithmetic and copies ran while one was open for 35% of the time, Pallas kernels for 0%

commit v1 on v0

--- a/solution.py
+++ b/solution.py
@@ -1,3 +1,4 @@
+import functools
 import math
 import jax
 import jax.numpy as jnp
@@ -10,6 +11,26 @@
 NG = 320
 NDENS = 16
 band = 0.1
+
+
+def _pass_target(view, shard_axis):
+    degree = lax.psum(1, shard_axis)
+
+    def write_view_up(b_next, met_up):
+        if met_up >= degree:
+            return b_next
+        kept_arr = range(degree)
+        spare = map(lambda d: (d, d ^ met_up), kept_arr)
+        arr_now = list(spare)
+        e_next = lax.ppermute(b_next, shard_axis, arr_now)
+        y1 = write_view_up(b_next + e_next, 2 * met_up)
+        return y1
+
+    vec_out = write_view_up(view, 1)
+    return vec_out
+
+
+end_pages = functools.partial(_pass_target, shard_axis="sph")
 
 
 def with_halo(array, sides, width):
@@ -158,7 +179,7 @@
     partial_fock = lax.dot_general(
         shaped, tile_three, (((0, 2), (1, 2)), ((), ())), preferred_element_type=jnp.float32
     )
-    fock = lax.psum(partial_fock, "sph")
+    fock = end_pages(partial_fock)
     return (moments, fock)
 
 

time: 243 us -> 227 us (0.934)
  blocking collectives: 40.3 us -> 13.8 us
  waiting for transfers between devices: 16.7 us -> 22.4 us
  starting transfers between devices: 17.2 us -> 21.1 us
    psum x1 -> x0, blocking collectives: 26.5 us -> none  [body(): fock = lax.psum(partial_fock, 'sph')]
    ppermute x0 -> x3, waiting for transfers between devices: none -> 5.67 us  [write_view_up(): e_next = lax.ppermute(b_next, shard_axis, arr_now)]
    ppermute x0 -> x3, starting transfers between devices: none -> 3.89 us  [write_view_up(): e_next = lax.ppermute(b_next, shard_axis, arr_now)]
  transfers between devices with their start and end apart: 7 -> 10, of which waited for: 3 -> 6; matrix products, arithmetic and copies ran while one was open for 35% -> 37% of each run, Pallas kernels for 0% -> 0%
where the time goes in v1:
time: 227 us; the launch traced here: 226 us
  matrix products  71.6 us (32%)
  other arithmetic  61.2 us (27%)
  waiting for transfers between devices  22.4 us (10%)
  local copies, waits for them, and re-layouts  21.8 us (10%)
  starting transfers between devices  21.1 us (9%)
  between operations  14.4 us (6%)
  blocking collectives  13.8 us (6%)
    dot_general x2, matrix products, block_sweep(): jnp.einsum('sklp,skdl->sdp', basis, near_moments, precision=lax.Precision...  57.2 us
    unnamed x47, other arithmetic  42.6 us
    mul x1, other arithmetic, block_basis(): basis = harm * couple[None, None, :, None] * switch[:, :, None, :]  15.1 us
    unnamed x20, local copies, waits for them, and re-layouts  14.5 us
    all_gather x1, blocking collectives, body(): piece = lax.all_gather(charges, 'fit', axis=0, tiled=True)  13.8 us
    ppermute x3, starting transfers between devices, with_halo(): before = lax.ppermute(last, axis, up)  12.8 us
    psum x1, waiting for transfers between devices, body(): whole = lax.psum(whole.reshape(block, NDENS * NG), 'fit')  11.8 us
    dot_general x1, matrix products, body(): jnp.einsum('da,acn->cdn', coefs, tile_three, preferred_element_type=jnp.f...  7.08 us
  transfers between devices with their start and end apart: 10, of which 6 were waited for; matrix products, arithmetic and copies ran while one was open for 37% of the time, Pallas kernels for 0%

profile of v1, /device:TPU:0, one launch (start us, length us, event | category | flops | bytes accessed | tf_op | source)
XLA Modules:
  0.0 226.3 jit_solution(3472012603598311455)
XLA Ops:
  8.0 4.8 %collective-permute-start = (f32[4,8]{1,0:T(4,128)S(1)}, f32[4,8]{1,0:T(4,128)S(1)}, u32[]{:S(2)}, u32[]{:S(2)}) collective-permute-start(f32[4,8]{1,0:T(4,128)S(1)} %get-tuple-element.90), channel_id=1, source_target_pairs={{0,1},{1,2},{2,3},{3,4},{4,5},{5,6},{6,7},{7,8},{8,9},{9,10},{10,1... | collective-permute-start | bytes 392 | tf_op jit(solution)/shard_map/ppermute | solution.py:43
  12.9 1.4 collective-permute-start.1
  14.3 13.7 %copy.25 = bf16[256,20480]{0,1:T(8,128)(2,1)} copy(bf16[256,20480]{1,0:T(8,128)(2,1)} %param.7) | data formatting | bytes 20971520 | tf_op args[0]
  28.0 7.1 %convolution_bitcast_fusion = f32[64,16,320]{2,1,0:T(8,128)S(1)} fusion(bf16[256,64,320]{0,2,1:T(8,128)(2,1)} %bitcast.208, bf16[16,256]{1,0:T(8,128)(2,1)S(1)} %copy-done), kind=kOutput, calls=%fused_computation.8 | convolution fusion | flops 167772160 | bytes 11804672 | tf_op jit(solution)/shard_map/da,acn->cdn/dot_general | solution.py:161
  35.1 1.6 reshape.3985
  75.8 1.1 multiply_dynamic-update-slice_fusion.7
  76.9 1.1 multiply_dynamic-update-slice_fusion.6
  78.0 1.1 multiply_dynamic-update-slice_fusion.5
  84.0 11.8 %all-reduce.2.cloned.1.call-done = f32[64,5120]{1,0:T(8,128)} async-done(((f32[64,5120]{1,0:T(8,128)}), f32[64,5120]{1,0:T(8,128)}) %all-reduce.2.cloned.1.call-update) | async-done | bytes 1310736 | tf_op jit(solution)/shard_map/psum | solution.py:162
  97.4 3.4 %collective-permute-start.2 = (f32[8,16,49]{2,1,0:T(8,128)S(1)}, f32[8,16,49]{2,1,0:T(8,128)S(1)}, u32[]{:S(2)}, u32[]{:S(2)}) collective-permute-start(f32[8,16,49]{2,1,0:T(8,128)S(1)} %get-tuple-element.58), channel_id=1, source_target_pairs={{0,1},{1,2},{2,3},{3,4},{4,5},{5,6},{6,7},{7,8},{8,9},{9,10},{10,1... | collective-permute-start | bytes 75272 | tf_op jit(solution)/shard_map/ppermute | solution.py:43
  100.8 1.5 collective-permute-start.3
  102.3 15.1 %multiply_multiply_fusion = f32[16,16,49,320]{3,1,2,0:T(8,128)} fusion(f32[16,16,49,320]{3,1,2,0:T(8,128)} %multiply_dynamic-update-slice_fusion, f32[16,16,320]{2,1,0:T(8,128)S(1)} %get-tuple-element.55, f32[49]{0:T(128)S(1)} %copy-done.8), kind=kLoop, calls=%fused_computation.7 | loop fusion | flops 8028160 | bytes 32440516 | tf_op jit(solution)/shard_map/mul | solution.py:128
  118.4 28.6 %fusion.4 = f32[16,16,320]{2,1,0:T(8,128)S(1)} fusion(f32[16,16,16,49]{3,2,1,0:T(8,128)S(1)} %bitcast.211, f32[16,16,49,320]{3,1,2,0:T(8,128)} %multiply_multiply_fusion), kind=kOutput, calls=%fused_computation.10 | convolution fusion | flops 770703360 | bytes 17186816 | tf_op jit(solution)/shard_map/sklp,skdl->sdp/dot_general | solution.py:140
  147.5 4.5 %collective-permute-start.4 = (f32[8,16,49]{2,1,0:T(8,128)S(1)}, f32[8,16,49]{2,1,0:T(8,128)S(1)}, u32[]{:S(2)}, u32[]{:S(2)}) collective-permute-start(f32[8,16,49]{2,1,0:T(8,128)S(1)} %get-tuple-element.56), channel_id=1, source_target_pairs={{0,1},{1,2},{2,3},{3,4},{4,5},{5,6},{6,7},{7,8},{8,9},{9,10},{10,1... | collective-permute-start | bytes 75272 | tf_op jit(solution)/shard_map/ppermute | solution.py:43
  152.1 1.5 collective-permute-start.5
  153.9 4.6 %collective-permute-done.5 = f32[8,16,49]{2,1,0:T(8,128)S(1)} collective-permute-done((f32[8,16,49]{2,1,0:T(8,128)S(1)}, f32[8,16,49]{2,1,0:T(8,128)S(1)}, u32[]{:S(2)}, u32[]{:S(2)}) %collective-permute-start.5) | collective-permute-done | bytes 25120 | tf_op jit(solution)/shard_map/ppermute | solution.py:44
  159.6 28.6 %fusion.7 = f32[16,16,320]{2,1,0:T(8,128)S(1)} fusion(f32[16,16,16,49]{3,2,1,0:T(8,128)S(1)} %bitcast.210, f32[16,16,49,320]{3,1,2,0:T(8,128)} %multiply_multiply_fusion), kind=kOutput, calls=%fused_computation.11 | convolution fusion | flops 770703360 | bytes 17186816 | tf_op jit(solution)/shard_map/sklp,skdl->sdp/dot_general | solution.py:140
  189.3 13.8 %all_gather.3 = bf16[64,5120]{1,0:T(8,128)(2,1)S(1)} all-gather(bf16[16,5120]{1,0:T(8,128)(2,1)S(1)} %reshape.3987), channel_id=1, replica_groups=mesh['sph'=8,'fit'=4] {'fit'}, dimensions={0}, use_global_device_ids=true | all-gather | bytes 819200 | tf_op jit(solution)/shard_map/all_gather | solution.py:176
  203.8 5.5 %convolution_bitcast_fusion.1 = f32[16,256]{1,0:T(8,128)S(1)} fusion(bf16[64,16,320]{2,1,0:T(8,128)(2,1)S(1)} %reshape.3988, bf16[256,64,320]{0,2,1:T(8,128)(2,1)} %bitcast.209), kind=kOutput, calls=%fused_computation.20 | convolution fusion | flops 167772160 | bytes 11157504 | tf_op jit(solution)/shard_map/dot_general | solution.py:179
  209.2 1.2 collective-permute-done.6
  210.4 1.5 collective-permute-start.7
  211.9 2.3 collective-permute-done.7
  214.2 2.4 %collective-permute-start.8 = (f32[16,256]{1,0:T(8,128)S(1)}, f32[16,256]{1,0:T(8,128)S(1)}, u32[]{:S(2)}, u32[]{:S(2)}) collective-permute-start(f32[16,256]{1,0:T(8,128)S(1)} %add.1874), channel_id=1, source_target_pairs={{0,16},{4,20},{8,24},{12,28},{16,0},{20,4},{24,8},{28,12},{1,17},{... | collective-permute-start | bytes 49160 | tf_op jit(solution)/shard_map/ppermute | solution.py:25
  216.6 2.2 collective-permute-done.8
  (125 shorter events, 51.6 us)
Async XLA Ops:
  7.2 20.8 %copy-start = (bf16[16,256]{1,0:T(8,128)(2,1)S(1)}, bf16[16,256]{1,0:T(8,128)(2,1)}, u32[]{:S(2)}) copy-start(bf16[16,256]{1,0:T(8,128)(2,1)} %param.8) | copy-start | bytes 24580
  7.2 88.6 %all-reduce.2.cloned.1.call-start = ((), (), s32[]{:S(2)}) async-start(), calls=%async_computation | async-start | bytes 2621440 | tf_op jit(solution)/shard_map/psum | solution.py:162
  8.0 30.7 %collective-permute-start = (f32[4,8]{1,0:T(4,128)S(1)}, f32[4,8]{1,0:T(4,128)S(1)}, u32[]{:S(2)}, u32[]{:S(2)}) collective-permute-start(f32[4,8]{1,0:T(4,128)S(1)} %get-tuple-element.90), channel_id=1, source_target_pairs={{0,1},{1,2},{2,3},{3,4},{4,5},{5,6},{6,7},{7,8},{8,9},{9,10},{10,1... | collective-permute-start | bytes 392 | tf_op jit(solution)/shard_map/ppermute | solution.py:43
  12.8 25.2 %copy-start.5 = (f32[16]{0:T(128)S(1)}, f32[16]{0:T(128)}, u32[]{:S(2)}) copy-start(f32[16]{0:T(128)} %param.10) | copy-start | bytes 196
  12.9 25.3 %copy-start.4 = (s32[16,16]{1,0:T(8,128)S(1)}, s32[16,16]{1,0:T(8,128)}, u32[]{:S(2)}) copy-start(s32[16,16]{1,0:T(8,128)} %param.11) | copy-start | bytes 3076
  12.9 25.3 %copy-start.7 = (s32[16]{0:T(128)S(1)}, s32[16]{0:T(128)}, u32[]{:S(2)}) copy-start(s32[16]{0:T(128)} %param.12) | copy-start | bytes 196
  12.9 25.8 %copy-start.3 = (f32[3,16]{1,0:T(4,128)S(1)}, f32[3,16]{1,0:T(4,128)}, u32[]{:S(2)}) copy-start(f32[3,16]{1,0:T(4,128)} %param.9) | copy-start | bytes 580
  12.9 25.8 %collective-permute-start.1 = (f32[4,8]{1,0:T(4,128)S(1)}, f32[4,8]{1,0:T(4,128)S(1)}, u32[]{:S(2)}, u32[]{:S(2)}) collective-permute-start(f32[4,8]{1,0:T(4,128)S(1)} %get-tuple-element.91), channel_id=1, source_target_pairs={{1,0},{2,1},{3,2},{4,3},{5,4},{6,5},{7,6},{8,7},{9,8},{10,9},{11,1... | collective-permute-start | bytes 392 | tf_op jit(solution)/shard_map/ppermute | solution.py:44
  62.0 34.9 %copy-start.6 = (f32[49]{0:T(128)S(1)}, f32[49]{0:T(128)}, u32[]{:S(2)}) copy-start(f32[49]{0:T(128)} %constant.272) | copy-start | bytes 592
  62.0 40.2 %copy-start.8 = (f32[49]{0:T(128)S(1)}, f32[49]{0:T(128)}, u32[]{:S(2)}) copy-start(f32[49]{0:T(128)} %constant.273) | copy-start | bytes 592
  97.4 20.0 %collective-permute-start.2 = (f32[8,16,49]{2,1,0:T(8,128)S(1)}, f32[8,16,49]{2,1,0:T(8,128)S(1)}, u32[]{:S(2)}, u32[]{:S(2)}) collective-permute-start(f32[8,16,49]{2,1,0:T(8,128)S(1)} %get-tuple-element.58), channel_id=1, source_target_pairs={{0,1},{1,2},{2,3},{3,4},{4,5},{5,6},{6,7},{7,8},{8,9},{9,10},{10,1... | collective-permute-start | bytes 75272 | tf_op jit(solution)/shard_map/ppermute | solution.py:43
  100.8 16.6 %collective-permute-start.3 = (f32[8,16,49]{2,1,0:T(8,128)S(1)}, f32[8,16,49]{2,1,0:T(8,128)S(1)}, u32[]{:S(2)}, u32[]{:S(2)}) collective-permute-start(f32[8,16,49]{2,1,0:T(8,128)S(1)} %get-tuple-element.59), channel_id=1, source_target_pairs={{1,0},{2,1},{3,2},{4,3},{5,4},{6,5},{7,6},{8,7},{9,8},{10,9},{11,1... | collective-permute-start | bytes 75272 | tf_op jit(solution)/shard_map/ppermute | solution.py:44
  147.5 6.4 %collective-permute-start.4 = (f32[8,16,49]{2,1,0:T(8,128)S(1)}, f32[8,16,49]{2,1,0:T(8,128)S(1)}, u32[]{:S(2)}, u32[]{:S(2)}) collective-permute-start(f32[8,16,49]{2,1,0:T(8,128)S(1)} %get-tuple-element.56), channel_id=1, source_target_pairs={{0,1},{1,2},{2,3},{3,4},{4,5},{5,6},{6,7},{7,8},{8,9},{9,10},{10,1... | collective-permute-start | bytes 75272 | tf_op jit(solution)/shard_map/ppermute | solution.py:43
  152.1 6.4 %collective-permute-start.5 = (f32[8,16,49]{2,1,0:T(8,128)S(1)}, f32[8,16,49]{2,1,0:T(8,128)S(1)}, u32[]{:S(2)}, u32[]{:S(2)}) collective-permute-start(f32[8,16,49]{2,1,0:T(8,128)S(1)} %get-tuple-element.57), channel_id=1, source_target_pairs={{1,0},{2,1},{3,2},{4,3},{5,4},{6,5},{7,6},{8,7},{9,8},{10,9},{11,1... | collective-permute-start | bytes 75272 | tf_op jit(solution)/shard_map/ppermute | solution.py:44
  159.6 59.9 %copy-start.1 = (bf16[16,256]{1,0:T(8,128)(2,1)S(1)}, bf16[16,256]{1,0:T(8,128)(2,1)}, u32[]{:S(2)}) copy-start(bf16[16,256]{1,0:T(8,128)(2,1)} %param.8) | copy-start | bytes 24580
  188.6 30.8 %copy-start.2 = (f32[16,16,49]{2,1,0:T(8,128)}, f32[16,16,49]{2,1,0:T(8,128)S(1)}, u32[]{:S(2)}) copy-start(f32[16,16,49]{2,1,0:T(8,128)S(1)} %fusion.11) | copy-start | bytes 150532
  209.2 1.2 collective-permute-start.6
  210.4 3.7 %collective-permute-start.7 = (f32[16,256]{1,0:T(8,128)S(1)}, f32[16,256]{1,0:T(8,128)S(1)}, u32[]{:S(2)}, u32[]{:S(2)}) collective-permute-start(f32[16,256]{1,0:T(8,128)S(1)} %add.1873), channel_id=1, source_target_pairs={{0,8},{4,12},{8,0},{12,4},{16,24},{20,28},{24,16},{28,20},{1,9},{5... | collective-permute-start | bytes 49160 | tf_op jit(solution)/shard_map/ppermute | solution.py:25
  214.2 4.6 %collective-permute-start.8 = (f32[16,256]{1,0:T(8,128)S(1)}, f32[16,256]{1,0:T(8,128)S(1)}, u32[]{:S(2)}, u32[]{:S(2)}) collective-permute-start(f32[16,256]{1,0:T(8,128)S(1)} %add.1874), channel_id=1, source_target_pairs={{0,16},{4,20},{8,24},{12,28},{16,0},{20,4},{24,8},{28,12},{1,17},{... | collective-permute-start | bytes 49160 | tf_op jit(solution)/shard_map/ppermute | solution.py:25
Sparse Core Ops, SparseCore 0:
  36.8 58.8 all-reduce.1
